TPU v7x, 256 devices: a whole 4x4x8 slice. The times are simulated.
256 devices in a mesh: dp: 4 (over y_lo, core), mp: 64 (over z, x, y_hi).
Axes of the slice: x: 4, y: 4 (y_hi: 2, y_lo: 2; y = y_hi * 2 + y_lo), z: 8, core: 2. Of those that a mesh axis runs over, the one named last changes fastest.
Arguments:
- features: bfloat16 [4096, 65536], P('dp', 'mp'), may hold values from -6 to 6
- cotangent: bfloat16 [4096, 65536], P('dp', 'mp'), may hold values from -6 to 6
- factor_one: bfloat16 [256, 256, 256], P('mp', 'dp'), may hold values from -0.375 to 0.375
- factor_two: bfloat16 [256, 256, 256], P('mp', 'dp'), may hold values from -0.375 to 0.375
Outputs:
- layer_out: bfloat16 [4096, 65536], P('dp', 'mp')
- grad_input: bfloat16 [4096, 65536], P('dp', 'mp')
- grad_one: float32 [256, 256, 256], P('mp', 'dp')
- grad_two: float32 [256, 256, 256], P('mp', 'dp')
All inputs are finite; a program needn't handle non-finite values.
Results may differ from a plain program's by a relative error of at most 0.0095.
Values may be sent and summed in bfloat16 or wider, within the bound.
A program may use at most 64 MiB of HBM per device.

v0:
```python
import math

import jax
import jax.numpy as jnp
from jax import lax
from jax.sharding import PartitionSpec as P

NB = 256
BS = 256


def gelu_value(value):
    inner = math.sqrt(2.0 / math.pi) * (value + 0.044715 * value * value * value)
    return 0.5 * value * (1.0 + jnp.tanh(inner))


def gelu_slope(value):
    scale = math.sqrt(2.0 / math.pi)
    tangent = jnp.tanh(scale * (value + 0.044715 * value * value * value))
    return 0.5 * (1.0 + tangent) + 0.5 * value * (1.0 - tangent * tangent) * scale * (
        1.0 + 3.0 * 0.044715 * value * value
    )


def on_device(features, cotangent, factor_one, factor_two):
    tokens = features.shape[0]
    groups = lax.axis_size("mp")
    w_one, w_two = (
        lax.all_gather(factor_one, "dp", axis=1, tiled=True),
        lax.all_gather(factor_two, "dp", axis=1, tiled=True),
    )
    blocks_in = features.reshape(tokens, NB // groups, BS)
    first = jnp.einsum("tbi,bij->bjt", blocks_in, w_one, preferred_element_type=jnp.float32).astype(
        jnp.bfloat16
    )
    mixed_in = lax.all_to_all(first, "mp", split_axis=1, concat_axis=0, tiled=True)
    preact = jnp.einsum("bjt,jbk->jkt", mixed_in, w_two, preferred_element_type=jnp.float32)
    pre_tokens = jnp.transpose(preact, (2, 0, 1))
    layer_out = (features.astype(jnp.float32) + gelu_value(pre_tokens).reshape(tokens, -1)).astype(
        jnp.bfloat16
    )
    cot_blocks = cotangent.reshape(tokens, BS // groups, NB).astype(jnp.float32)
    slope = (cot_blocks * gelu_slope(pre_tokens)).astype(jnp.bfloat16)
    back_mixed = jnp.einsum(
        "tjk,jbk->bjt", slope, w_two, preferred_element_type=jnp.float32
    ).astype(jnp.bfloat16)
    back_first = lax.all_to_all(back_mixed, "mp", split_axis=0, concat_axis=1, tiled=True)
    through = jnp.einsum("bjt,bij->tbi", back_first, w_one, preferred_element_type=jnp.float32)
    grad_input = (cotangent.astype(jnp.float32) + through.reshape(tokens, -1)).astype(jnp.bfloat16)
    part_two = jnp.einsum("bjt,tjk->jbk", mixed_in, slope, preferred_element_type=jnp.float32)
    part_one = jnp.einsum("tbi,bjt->bij", blocks_in, back_first, preferred_element_type=jnp.float32)
    grad_one, grad_two = (
        lax.psum_scatter(
            part_one.astype(jnp.bfloat16), "dp", scatter_dimension=1, tiled=True
        ).astype(jnp.float32),
        lax.psum_scatter(
            part_two.astype(jnp.bfloat16), "dp", scatter_dimension=1, tiled=True
        ).astype(jnp.float32),
    )
    return (layer_out, grad_input, grad_one, grad_two)


def solution(mesh):
    in_specs = (P("dp", "mp"), P("dp", "mp"), P("mp", "dp", None), P("mp", "dp", None))
    out_specs = (P("dp", "mp"), P("dp", "mp"), P("mp", "dp", None), P("mp", "dp", None))
    return jax.shard_map(
        on_device, mesh=mesh, in_specs=in_specs, out_specs=out_specs, check_vma=False
    )
```

profile of v0, /device:TPU:1, one launch (start us, length us, event | category | flops | bytes accessed | tf_op | source)
XLA Modules:
  0.0 220.5 jit_solution(12188736925813567215)
XLA Ops:
  7.2 9.8 %all_gather.6 = bf16[4,256,256]{2,1,0:T(8,128)(2,1)S(1)} all-gather(bf16[4,64,256]{2,1,0:T(8,128)(2,1)} %param.6), channel_id=1, replica_groups=mesh['dp'=4,'mp'=64] {'dp'}, dimensions={1}, use_global_device_ids=true | all-gather | bytes 655360 | tf_op jit(solution)/shard_map/all_gather | solution.py:29
  16.9 2.4 %fusion.12 = bf16[4,256,1024]{2,1,0:T(8,128)(2,1)S(1)} fusion(bf16[4,256,256]{2,1,0:T(8,128)(2,1)S(1)} %all_gather.6, bf16[128,4,8,256]{3,2,1,0:T(8,128)(2,1)} %bitcast.57), kind=kOutput, calls=%fused_computation.19 | convolution fusion | flops 537919488 | bytes 4718592 | tf_op jit(solution)/shard_map/tbi,bij->bjt/dot_general | solution.py:33
  19.3 2.9 %copy.30 = bf16[4,256,1024]{2,0,1:T(4,128)(2,1)} copy(bf16[4,256,1024]{2,1,0:T(8,128)(2,1)S(1)} %fusion.12) | data formatting | bytes 4194304 | tf_op jit(solution)/shard_map/convert_element_type | solution.py:33
  22.2 13.0 %all-to-all-start = ((bf16[4,256,1024]{2,0,1:T(4,128)(2,1)}), bf16[4,256,1024]{2,0,1:T(4,128)(2,1)S(1)}, u32[]{:S(2)}, u32[]{:S(2)}) async-start(bf16[4,256,1024]{2,0,1:T(4,128)(2,1)} %copy.30), calls=%async_computation | async-start | bytes 4194304 | tf_op jit(solution)/shard_map/all_to_all | solution.py:36
  35.3 4.2 %copy.33 = f32[1024,1024]{0,1:T(8,128)} copy(bf16[1024,1024]{1,0:T(8,128)(2,1)} %param.5) | data formatting | bytes 6291456 | tf_op jit(solution)/shard_map/convert_element_type | solution.py:49
  39.5 9.4 %all_gather.7 = bf16[4,256,256]{2,1,0:T(8,128)(2,1)S(1)} all-gather(bf16[4,64,256]{2,1,0:T(8,128)(2,1)S(1)} %copy-done.3), channel_id=1, replica_groups=mesh['dp'=4,'mp'=64] {'dp'}, dimensions={1}, use_global_device_ids=true | all-gather | bytes 655360 | tf_op jit(solution)/shard_map/all_gather | solution.py:30
  48.8 36.4 %all-to-all-done = bf16[4,256,1024]{2,0,1:T(4,128)(2,1)S(1)} async-done(((bf16[4,256,1024]{2,0,1:T(4,128)(2,1)}), bf16[4,256,1024]{2,0,1:T(4,128)(2,1)S(1)}, u32[]{:S(2)}, u32[]{:S(2)}) %all-to-all-start) | async-done | bytes 2097184 | tf_op jit(solution)/shard_map/all_to_all | solution.py:36
  85.2 2.1 copy.58
  87.3 2.5 %all_to_all.29 = bf16[256,4,1024]{2,0,1:T(8,128)(2,1)S(1)} reshape(bf16[64,4,4,1024]{3,1,0,2:T(4,128)(2,1)} %bitcast.56) | data formatting | bytes 4194304 | tf_op jit(solution)/shard_map/all_to_all | solution.py:36
  89.9 7.0 %fusion.6 = (bf16[1024,4,256]{0,2,1:T(8,128)(2,1)S(1)}, f32[1024,4,256]{0,2,1:T(8,128)}) fusion(f32[1024,4,256]{0,2,1:T(8,128)} %bitcast.59, bf16[256,4,1024]{2,0,1:T(8,128)(2,1)S(1)} %all_to_all.29, bf16[4,256,256]{2,1,0:T(8,128)(2,1)S(1)} %all_gather.7), kind=kOutput, calls=%fused_computation.8 | convolution fusion | flops 557842432 | bytes 13107200 | tf_op jit(solution)/shard_map/bjt,jbk->jkt/dot_general | solution.py:37
  96.9 1.3 copy-done.2
  98.2 1.0 convert_bitcast_fusion
  99.2 3.1 %copy.35 = bf16[256,4,1024]{2,1,0:T(4,128)(2,1)} copy(bf16[256,4,1024]{0,2,1:T(8,128)(2,1)S(1)} %convert_bitcast_fusion) | data formatting | bytes 4194304 | tf_op jit(solution)/shard_map/convert_element_type | solution.py:46
  102.3 7.8 %all-to-all-start.1 = ((bf16[256,4,1024]{2,1,0:T(4,128)(2,1)}), bf16[256,4,1024]{2,1,0:T(4,128)(2,1)S(1)}, u32[]{:S(2)}, u32[]{:S(2)}) async-start(bf16[256,4,1024]{2,1,0:T(4,128)(2,1)} %copy.35), calls=%async_computation.1 | async-start | bytes 4194304 | tf_op jit(solution)/shard_map/all_to_all | solution.py:47
  110.1 0.0 reduce-scatter.2.cloned.1.call-start
  110.1 3.8 %convolution_convert_fusion = bf16[4,256,256]{2,1,0:T(8,128)(2,1)} fusion(bf16[256,4,1024]{2,0,1:T(8,128)(2,1)} %copy-done.1, bf16[1024,4,256]{0,2,1:T(8,128)(2,1)} %copy-done.2), kind=kOutput, calls=%fused_computation.23 | convolution fusion | flops 537133056 | bytes 4718592 | tf_op jit(solution)/shard_map/bjt,tjk->jbk/dot_general | solution.py:50
  113.9 0.2 all-reduce.3.cloned.1.call-start
  114.2 0.6 dynamic-slice
  115.4 5.4 %copy.32 = f32[1024,1024]{1,0:T(8,128)} copy(f32[1024,1024]{0,1:T(8,128)} %bitcast.60) | data formatting | bytes 8388608 | tf_op jit(solution)/shard_map/reshape | solution.py:39
  120.8 18.8 %reduce-scatter.2.cloned.1.call-done = bf16[4,64,256]{2,1,0:T(8,128)(2,1)} async-done(((bf16[4,256,256]{2,1,0:T(8,128)(2,1)}), bf16[4,64,256]{2,1,0:T(8,128)(2,1)}) %reduce-scatter.2.cloned.1.call-update) | async-done | bytes 131088 | tf_op jit(solution)/shard_map/reduce_scatter | solution.py:56
  139.6 1.6 convert_element_type.59
  141.3 17.0 %all-to-all-done.1 = bf16[256,4,1024]{2,1,0:T(4,128)(2,1)S(1)} async-done(((bf16[256,4,1024]{2,1,0:T(4,128)(2,1)}), bf16[256,4,1024]{2,1,0:T(4,128)(2,1)S(1)}, u32[]{:S(2)}, u32[]{:S(2)}) %all-to-all-start.1) | async-done | bytes 2097184 | tf_op jit(solution)/shard_map/all_to_all | solution.py:47
  158.3 2.1 copy.36
  160.4 2.5 %all_to_all.33 = bf16[4,256,1024]{2,1,0:T(8,128)(2,1)S(1)} reshape(bf16[4,64,4,1024]{3,2,1,0:T(4,128)(2,1)} %copy.36) | data formatting | bytes 4194304 | tf_op jit(solution)/shard_map/all_to_all | solution.py:47
  163.0 2.3 %fusion.20 = bf16[4,256,256]{1,2,0:T(8,128)(2,1)S(1)} fusion(bf16[4,256,1024]{2,1,0:T(8,128)(2,1)S(1)} %all_to_all.33, bf16[128,4,8,256]{3,2,1,0:T(8,128)(2,1)} %bitcast.58), kind=kOutput, calls=%fused_computation.24 | convolution fusion | flops 537133056 | bytes 4718592 | tf_op jit(solution)/shard_map/tbi,bjt->bij/dot_general | solution.py:51
  165.3 2.7 %fusion.23 = f32[4,1024,256]{1,2,0:T(8,128)} fusion(bf16[4,256,256]{2,1,0:T(8,128)(2,1)S(1)} %all_gather.6, bf16[4,256,1024]{2,1,0:T(8,128)(2,1)S(1)} %all_to_all.33), kind=kOutput, calls=%fused_computation.26 | convolution fusion | flops 536870912 | bytes 6815744 | tf_op jit(solution)/shard_map/bjt,bij->tbi/dot_general | solution.py:48
  168.0 1.1 copy.39
  169.1 5.5 %copy.37 = f32[1024,1024]{1,0:T(8,128)} copy(f32[1024,1024]{0,1:T(8,128)} %bitcast.53) | data formatting | bytes 8388608 | tf_op jit(solution)/shard_map/reshape | solution.py:49
  174.6 7.6 %add_convert_fusion = (bf16[1024,1024]{1,0:T(8,128)(2,1)}, bf16[1024,1024]{1,0:T(8,128)(2,1)}) fusion(f32[1024,1024]{1,0:T(8,128)} %copy.37, bf16[1024,1024]{1,0:T(8,128)(2,1)S(1)} %copy-done, f32[1024,1024]{1,0:T(8,128)} %copy.32, bf16[1024,1024]{1,0:T(8,128)(2,1)} %param.4), kind=kLoop, calls=%fused_computation.10 | loop fusion | flops 6291456 | bytes 16777216 | tf_op jit(solution)/shard_map/convert_element_type | solution.py:49
  182.2 29.8 %all-reduce.3.cloned.1.call-done = bf16[4,256,256]{2,0,1:T(4,128)(2,1)} async-done(((bf16[4,256,256]{2,0,1:T(4,128)(2,1)}), bf16[4,256,256]{2,0,1:T(4,128)(2,1)}) %all-reduce.3.cloned.1.call-update) | async-done | bytes 524304
  212.0 0.9 dynamic-slice_convert_fusion
  212.9 0.8 copy.41
  (11 shorter events, 0.1 us)
Async XLA Ops:
  22.2 63.0 %all-to-all-start = ((bf16[4,256,1024]{2,0,1:T(4,128)(2,1)}), bf16[4,256,1024]{2,0,1:T(4,128)(2,1)S(1)}, u32[]{:S(2)}, u32[]{:S(2)}) async-start(bf16[4,256,1024]{2,0,1:T(4,128)(2,1)} %copy.30), calls=%async_computation | async-start | bytes 4194304 | tf_op jit(solution)/shard_map/all_to_all | solution.py:36
  35.3 4.2 %copy-start.3 = (bf16[4,64,256]{2,1,0:T(8,128)(2,1)S(1)}, bf16[4,64,256]{2,1,0:T(8,128)(2,1)}, u32[]{:S(2)}) copy-start(bf16[4,64,256]{2,1,0:T(8,128)(2,1)} %param.7) | copy-start | bytes 393220
  89.9 7.1 %copy-start.1 = (bf16[256,4,1024]{2,0,1:T(8,128)(2,1)}, bf16[256,4,1024]{2,0,1:T(8,128)(2,1)S(1)}, u32[]{:S(2)}) copy-start(bf16[256,4,1024]{2,0,1:T(8,128)(2,1)S(1)} %all_to_all.29) | copy-start | bytes 6291460
  96.9 1.3 copy-start.2
  102.3 56.0 %all-to-all-start.1 = ((bf16[256,4,1024]{2,1,0:T(4,128)(2,1)}), bf16[256,4,1024]{2,1,0:T(4,128)(2,1)S(1)}, u32[]{:S(2)}, u32[]{:S(2)}) async-start(bf16[256,4,1024]{2,1,0:T(4,128)(2,1)} %copy.35), calls=%async_computation.1 | async-start | bytes 4194304 | tf_op jit(solution)/shard_map/all_to_all | solution.py:47
  110.1 4.1 %copy-start.4 = (u32[256]{0:T(256)S(1)}, u32[256]{0:T(256)}, u32[]{:S(2)}) copy-start(u32[256]{0:T(256)} %constant.14) | copy-start | bytes 3076
  110.1 29.6 %reduce-scatter.2.cloned.1.call-start = ((), (), s32[]{:S(2)}) async-start(), calls=%async_computation.3 | async-start | bytes 655360 | tf_op jit(solution)/shard_map/reduce_scatter | solution.py:56
  113.9 98.1 %all-reduce.3.cloned.1.call-start = ((), (), s32[]{:S(2)}) async-start(), calls=%async_computation.4 | async-start | bytes 1048576
  169.1 5.5 %copy-start = (bf16[1024,1024]{1,0:T(8,128)(2,1)S(1)}, bf16[1024,1024]{1,0:T(8,128)(2,1)}, u32[]{:S(2)}) copy-start(bf16[1024,1024]{1,0:T(8,128)(2,1)} %param.5) | copy-start | bytes 6291460
Sparse Core Ops, SparseCore 0:
  114.0 25.5 reduce-scatter.1
  169.2 42.7 all-reduce.2
where the time goes:
time: 221 us
  waiting for transfers between devices  102 us (46%)
  local copies, waits for them, and re-layouts  34.2 us (15%)
  starting transfers between devices  21.1 us (10%)
  blocking collectives  19.1 us (9%)
  matrix products  19.1 us (9%)
  between operations  14.8 us (7%)
  other arithmetic  10.2 us (5%)
    all_to_all x1, waiting for transfers between devices, on_device(): lax.all_to_all(first, 'mp', split_axis=1, concat_axis=0, tiled=True)  36.4 us
    unnamed x3, waiting for transfers between devices  29.8 us
    reduce_scatter x1, waiting for transfers between devices, on_device(): lax.psum_scatter(part_two.astype(jnp.bfloat16), 'dp', scatter_dimension=1...  18.8 us
    all_to_all x1, waiting for transfers between devices, on_device(): lax.all_to_all(back_mixed, 'mp', split_axis=0, concat_axis=1, tiled=True)  17 us
    all_to_all x1, starting transfers between devices, on_device(): lax.all_to_all(first, 'mp', split_axis=1, concat_axis=0, tiled=True)  13 us
    all_gather x1, blocking collectives, on_device(): lax.all_gather(factor_one, 'dp', axis=1, tiled=True)  9.75 us
    all_gather x1, blocking collectives, on_device(): lax.all_gather(factor_two, 'dp', axis=1, tiled=True)  9.36 us
    all_to_all x1, starting transfers between devices, on_device(): lax.all_to_all(back_mixed, 'mp', split_axis=0, concat_axis=1, tiled=True)  7.76 us
  transfers between devices with their start and end apart: 4, of which 4 were waited for; matrix products, arithmetic and copies ran while one was open for 13% of the time, Pallas kernels for 0%

commit v1 on v0

v1 whole, which is shorter than its diff:
```python
import functools
import math

import jax
import jax.numpy as jnp
from jax import lax
from jax.experimental import pallas as pl
from jax.experimental.pallas import tpu as pltpu
from jax.sharding import PartitionSpec as P

MESH = pl.DeviceIdType.MESH
BF16 = jnp.bfloat16
F32 = jnp.float32
CHUNKS = 4

NT = (((1,), (1,)), ((), ()))
TN = (((0,), (0,)), ((), ()))
NN = (((1,), (0,)), ((), ()))


def dot(a, b, dims):
    return lax.dot_general(a, b, dims, preferred_element_type=F32)


def gelu_both(v):
    scale = math.sqrt(2.0 / math.pi)
    sq = v * v
    t = jnp.tanh(scale * (v + 0.044715 * sq * v))
    half = 0.5 * (1.0 + t)
    value = v * half
    slope = half + 0.5 * v * (1.0 - t * t) * scale * (1.0 + 3.0 * 0.044715 * sq)
    return value, slope


def kernel(
    groups,
    shards,
    x_hbm,
    c_hbm,
    w1_hbm,
    w2_hbm,
    lay_hbm,
    gin_hbm,
    g1_hbm,
    g2_hbm,
    x_ref,
    c_ref,
    lay_ref,
    gin_ref,
    slope_ref,
    w1_ref,
    w2_ref,
    w1x_ref,
    w2x_ref,
    perm_ref,
    pick_ref,
    s1_ref,
    r1_ref,
    s2_ref,
    r2_ref,
    f_ref,
    acc1_ref,
    acc2_ref,
    p1_ref,
    p2_ref,
    q1_ref,
    q2_ref,
    o1_ref,
    o2_ref,
    in_sem,
    w_sem,
    send_sem,
    r1_sem,
    r2_sem,
    q_sem,
    out_sem,
):
    me = lax.axis_index("mp")
    my = lax.axis_index("dp")
    tokens, width = x_ref.shape
    local = width // 256
    tc = tokens // CHUNKS
    own = 256 // shards
    rows = local * local

    load_x = pltpu.make_async_copy(x_hbm, x_ref, in_sem.at[0])
    load_c = pltpu.make_async_copy(c_hbm, c_ref, in_sem.at[1])
    load_x.start()
    load_c.start()

    barrier = pltpu.get_barrier_semaphore()

    def greet(step, _):
        pl.semaphore_signal(
            barrier, inc=1, device_id=(my, lax.rem(me + step, groups)), device_id_type=MESH
        )
        return 0

    def greet_dp(step, _):
        pl.semaphore_signal(
            barrier, inc=1, device_id=(lax.rem(my + step, shards), me), device_id_type=MESH
        )
        return 0

    lax.fori_loop(1, shards, greet_dp, 0)
    lax.fori_loop(1, groups, greet, 0)

    def build(i, _):
        r0 = pl.multiple_of(i * 128, 128)
        row = lax.broadcasted_iota(jnp.int32, (128, 256), 0) + r0
        col = lax.broadcasted_iota(jnp.int32, (128, 256), 1)
        m4 = lax.shift_right_logical(row, 4) * 4
        u = lax.bitwise_and(lax.shift_right_logical(row, 2), 3)
        v = lax.bitwise_and(row, 3)
        for q in range(local):
            pick_ref[pl.ds(r0, 128), q * 256 : (q + 1) * 256] = jnp.where(
                jnp.logical_and(v == q, col == m4 + u), 1.0, 0.0
            ).astype(BF16)
            perm_ref[pl.ds(r0, 128), q * 256 : (q + 1) * 256] = jnp.where(
                jnp.logical_and(u == q, col == m4 + v), 1.0, 0.0
            ).astype(BF16)
        return 0

    lax.fori_loop(0, width // 128, build, 0)

    pl.semaphore_wait(barrier, groups - 1 + shards - 1)

    mine = pl.ds(pl.multiple_of(my * own, own), own)
    for n, (w_hbm, w_ref) in enumerate(((w1_hbm, w1_ref), (w2_hbm, w2_ref))):
        pltpu.make_async_copy(w_hbm, w_ref.at[:, mine, :], w_sem.at[n]).start()
        for step in range(1, shards):
            pltpu.make_async_remote_copy(
                src_ref=w_hbm,
                dst_ref=w_ref.at[:, mine, :],
                send_sem=send_sem.at[n],
                recv_sem=w_sem.at[n],
                device_id=(lax.rem(my + step, shards), me),
                device_id_type=MESH,
            ).start()

    def scatter(src, dst, c, ssem, rsem):
        here = pl.ds(pl.multiple_of(me * rows, rows), rows)
        pltpu.make_async_copy(src.at[c, here, :], dst.at[c, here, :], rsem.at[c]).start()

        def send(step, _):
            to = lax.rem(me + step, groups)
            pltpu.make_async_remote_copy(
                src_ref=src.at[c, pl.ds(pl.multiple_of(to * rows, rows), rows), :],
                dst_ref=dst.at[c, here, :],
                send_sem=ssem,
                recv_sem=rsem.at[c],
                device_id=(my, to),
                device_id_type=MESH,
            ).start()
            return 0

        lax.fori_loop(1, groups, send, 0)

    def expand(out_ref, w_ref, dims):
        for q in range(local):
            w = w_ref[q]
            for i in range(4):
                part = slice(i * 256, (i + 1) * 256)
                out_ref[part, q * 256 : (q + 1) * 256] = dot(
                    pick_ref[part, q * 256 : (q + 1) * 256], w, dims
                ).astype(BF16)

    load_x.wait()
    pltpu.make_async_copy(w1_ref, w1_ref, w_sem.at[0]).wait()
    expand(w1x_ref, w1_ref, NT)

    def first_stage(c, _):
        here = pl.ds(pl.multiple_of(c * tc, tc), tc)
        for i in range(4):
            part = slice(i * 256, (i + 1) * 256)
            s1_ref[c, part, :] = dot(w1x_ref[part, :], x_ref[here, :], NT).astype(BF16)
        scatter(s1_ref, r1_ref, c, send_sem.at[2], r1_sem)
        return 0

    lax.fori_loop(0, CHUNKS, first_stage, 0)

    pltpu.make_async_copy(w2_ref, w2_ref, w_sem.at[1]).wait()
    expand(w2x_ref, w2_ref, NN)
    acc1_ref[...] = jnp.zeros_like(acc1_ref)
    acc2_ref[...] = jnp.zeros_like(acc2_ref)
    load_c.wait()

    def second_stage(c, _):
        here = pl.ds(pl.multiple_of(c * tc, tc), tc)
        pltpu.make_async_copy(r1_ref.at[c], r1_ref.at[c], r1_sem.at[c]).wait()
        got = r1_ref[c].T
        for q in range(local):
            cols = slice(q * 256, (q + 1) * 256)
            f = dot(got, perm_ref[:, cols], NN).astype(BF16)
            f_ref[:, cols] = f
            pre = dot(f, w2_ref[q], NN)
            value, slope = gelu_both(pre)
            lay_ref[here, cols] = (x_ref[here, cols].astype(F32) + value).astype(BF16)
            slope_ref[here, cols] = (c_ref[here, cols].astype(F32) * slope).astype(BF16)
        for i in range(4):
            part = slice(i * 256, (i + 1) * 256)
            s2_ref[c, part, :] = dot(w2x_ref[part, :], slope_ref[here, :], NT).astype(BF16)
        scatter(s2_ref, r2_ref, c, send_sem.at[3], r2_sem)
        pltpu.make_async_copy(lay_ref.at[here, :], lay_hbm.at[here, :], out_sem.at[0]).start()
        for q in range(local):
            cols = slice(q * 256, (q + 1) * 256)
            acc2_ref[q] += dot(f_ref[:, cols], slope_ref[here, cols], TN)
        return 0

    lax.fori_loop(0, CHUNKS, second_stage, 0)

    def reduce_start(n, acc_ref, p_ref, q_ref):
        p_ref[...] = acc_ref[...].astype(BF16)
        pltpu.make_async_copy(p_ref.at[:, mine, :], q_ref.at[my], q_sem.at[n]).start()
        for step in range(1, shards):
            to = lax.rem(my + step, shards)
            pltpu.make_async_remote_copy(
                src_ref=p_ref.at[:, pl.ds(pl.multiple_of(to * own, own), own), :],
                dst_ref=q_ref.at[my],
                send_sem=send_sem.at[4 + n],
                recv_sem=q_sem.at[n],
                device_id=(to, me),
                device_id_type=MESH,
            ).start()

    def reduce_end(n, q_ref, o_ref, g_hbm):
        pltpu.make_async_copy(q_ref, q_ref, q_sem.at[n]).wait()
        total = q_ref[0].astype(F32)
        for s in range(1, shards):
            total = total + q_ref[s].astype(F32)
        o_ref[...] = total
        pltpu.make_async_copy(o_ref, g_hbm, out_sem.at[2 + n]).start()

    reduce_start(1, acc2_ref, p2_ref, q2_ref)

    def last_stage(c, _):
        here = pl.ds(pl.multiple_of(c * tc, tc), tc)
        pltpu.make_async_copy(r2_ref.at[c], r2_ref.at[c], r2_sem.at[c]).wait()
        got = r2_ref[c].T
        for q in range(local):
            cols = slice(q * 256, (q + 1) * 256)
            f = dot(got, perm_ref[:, cols], NN).astype(BF16)
            acc1_ref[q] += dot(x_ref[here, cols], f, TN)
            through = dot(f, w1_ref[q], NT)
            gin_ref[here, cols] = (c_ref[here, cols].astype(F32) + through).astype(BF16)
        pltpu.make_async_copy(gin_ref.at[here, :], gin_hbm.at[here, :], out_sem.at[1]).start()
        return 0

    lax.fori_loop(0, CHUNKS - 1, last_stage, 0)
    reduce_end(1, q2_ref, o2_ref, g2_hbm)
    last_stage(CHUNKS - 1, 0)
    reduce_start(0, acc1_ref, p1_ref, q1_ref)
    reduce_end(0, q1_ref, o1_ref, g1_hbm)

    for n, w_hbm in enumerate((w1_hbm, w2_hbm)):
        for _ in range(1, shards):
            pltpu.make_async_copy(w_hbm, w_hbm, send_sem.at[n]).wait()
    others = pl.ds(0, (groups - 1) * rows)
    for n, s_ref in ((2, s1_ref), (3, s2_ref)):
        for c in range(CHUNKS):
            pltpu.make_async_copy(
                s_ref.at[c, others, :], s_ref.at[c, others, :], send_sem.at[n]
            ).wait()
    for n, p_ref in enumerate((p1_ref, p2_ref)):
        part = p_ref.at[:, pl.ds(0, (shards - 1) * own), :]
        pltpu.make_async_copy(part, part, send_sem.at[4 + n]).wait()
    pltpu.make_async_copy(lay_ref, lay_hbm, out_sem.at[0]).wait()
    pltpu.make_async_copy(gin_ref, gin_hbm, out_sem.at[1]).wait()
    pltpu.make_async_copy(o1_ref, g1_hbm, out_sem.at[2]).wait()
    pltpu.make_async_copy(o2_ref, g2_hbm, out_sem.at[3]).wait()


def on_device(features, cotangent, factor_one, factor_two):
    groups, shards = lax.axis_size("mp"), lax.axis_size("dp")
    tokens, width = features.shape
    tc = tokens // CHUNKS
    local = width // 256
    big = pltpu.VMEM((tokens, width), BF16)
    square = pltpu.VMEM((width, width), BF16)
    message = pltpu.VMEM((CHUNKS, width, tc), BF16)
    blocks = (local, 256, 256)
    anywhere = pl.BlockSpec(memory_space=pl.ANY)
    return pl.pallas_call(
        functools.partial(kernel, groups, shards),
        out_shape=(
            jax.ShapeDtypeStruct(features.shape, BF16),
            jax.ShapeDtypeStruct(features.shape, BF16),
            jax.ShapeDtypeStruct(factor_one.shape, F32),
            jax.ShapeDtypeStruct(factor_two.shape, F32),
        ),
        in_specs=[anywhere] * 4,
        out_specs=(anywhere,) * 4,
        scratch_shapes=[
            big,
            big,
            big,
            big,
            big,
            pltpu.VMEM(blocks, BF16),
            pltpu.VMEM(blocks, BF16),
            square,
            square,
            square,
            square,
            message,
            message,
            message,
            message,
            pltpu.VMEM((tc, width), BF16),
            pltpu.VMEM(blocks, F32),
            pltpu.VMEM(blocks, F32),
            pltpu.VMEM(blocks, BF16),
            pltpu.VMEM(blocks, BF16),
            pltpu.VMEM((shards,) + factor_one.shape, BF16),
            pltpu.VMEM((shards,) + factor_one.shape, BF16),
            pltpu.VMEM(factor_one.shape, F32),
            pltpu.VMEM(factor_one.shape, F32),
            pltpu.SemaphoreType.DMA((2,)),
            pltpu.SemaphoreType.DMA((2,)),
            pltpu.SemaphoreType.DMA((6,)),
            pltpu.SemaphoreType.DMA((CHUNKS,)),
            pltpu.SemaphoreType.DMA((CHUNKS,)),
            pltpu.SemaphoreType.DMA((2,)),
            pltpu.SemaphoreType.DMA((4,)),
        ],
        compiler_params=pltpu.CompilerParams(
            collective_id=0, has_side_effects=True, vmem_limit_bytes=56 * 2**20
        ),
        name="monarch",
    )(features, cotangent, factor_one, factor_two)


def solution(mesh):
    in_specs = (P("dp", "mp"), P("dp", "mp"), P("mp", "dp", None), P("mp", "dp", None))
    out_specs = (P("dp", "mp"), P("dp", "mp"), P("mp", "dp", None), P("mp", "dp", None))
    return jax.shard_map(
        on_device, mesh=mesh, in_specs=in_specs, out_specs=out_specs, check_vma=False
    )
```

time: 221 us -> 131 us (0.59); the launches traced: 221 us -> 128 us
  Pallas kernels: 0 us -> 122 us
  waiting for transfers between devices: 102 us -> 0 us
  local copies, waits for them, and re-layouts: 34.2 us -> 5.96 us
  starting transfers between devices: 21.1 us -> 0 us
  matrix products: 19.1 us -> 0 us
  blocking collectives: 19.1 us -> 0 us
  between operations: 14.8 us -> 0.65 us
  other arithmetic: 10.2 us -> 0 us
    pallas_call x0 -> x1, Pallas kernels: none -> 122 us  [on_device(): pl.pallas_call(functools.partial(kernel, groups, shards), out_shape=(jax....]
    all_to_all x2 -> x0, waiting for transfers between devices: 53.4 us -> none  [the longest x1 36.4 us: on_device(): lax.all_to_all(first, 'mp', split_axis=1, concat_axis=0, tiled=True)]
    unnamed x3 -> x0, waiting for transfers between devices: 29.8 us -> none
    all_to_all x2 -> x0, starting transfers between devices: 20.8 us -> none  [the longest x1 13 us: on_device(): lax.all_to_all(first, 'mp', split_axis=1, concat_axis=0, tiled=True)]
    dot_general x6 -> x0, matrix products: 19.1 us -> none  [the longest x1 7.04 us: on_device(): jnp.einsum('bjt,jbk->jkt', mixed_in, w_two, preferred_element_type=jnp.fl...]
    all_gather x2 -> x0, blocking collectives: 19.1 us -> none  [the longest x1 9.75 us: on_device(): lax.all_gather(factor_one, 'dp', axis=1, tiled=True)]
    reduce_scatter x1 -> x0, waiting for transfers between devices: 18.8 us -> none  [on_device(): lax.psum_scatter(part_two.astype(jnp.bfloat16), 'dp', scatter_dimension=1...]
    convert_element_type x4 -> x0, local copies, waits for them, and re-layouts: 11.3 us -> none  [the longest x1 4.18 us: on_device(): cotangent.astype(jnp.float32) + through.reshape(tokens, -1)]
  transfers between devices with their start and end apart: 4 -> 0, of which waited for: 4 -> 0; matrix products, arithmetic and copies ran while one was open for 13% -> 0% of each run, Pallas kernels for 0% -> 0%
where the time goes in v1:
time: 131 us; the launch traced here: 128 us
  Pallas kernels  122 us (93%)
  local copies, waits for them, and re-layouts  5.96 us (5%)
    pallas_call x1, Pallas kernels, on_device(): pl.pallas_call(functools.partial(kernel, groups, shards), out_shape=(jax....  122 us
    unnamed x10, local copies, waits for them, and re-layouts  5.96 us

profile of v1, /device:TPU:1, one launch (start us, length us, event | category | flops | bytes accessed | tf_op | source)
XLA Modules:
  0.0 128.2 jit_solution(411353651439174380)
XLA Ops:
  0.6 121.6 %monarch.1 = (bf16[1024,1024]{1,0:T(8,128)(2,1)}, bf16[1024,1024]{1,0:T(8,128)(2,1)}, f32[4,64,256]{2,1,0:T(8,128)}, f32[4,64,256]{2,1,0:T(8,128)}) custom-call(bf16[1024,1024]{1,0:T(8,128)(2,1)} %x_hbm.1, bf16[1024,1024]{1,0:T(8,128)(2,1)} %c_hbm.1, bf16[4,64,256]{2,1,0:T(8,128)(2,1)} %w1_hbm.1, bf16[4,64,256]{2,1,0:T(8,128)(2,1)} %w2_hbm.1), custom_call_target="tpu_custom_call" | custom-call | tf_op jit(solution)/shard_map/monarch/pallas_call | solution.py:283
  122.2 0.0 copy-start
  122.2 3.2 %copy.12 = bf16[1024,1024]{1,0:T(8,128)(2,1)} copy(bf16[1024,1024]{1,0:T(8,128)(2,1)} %get-tuple-element.8) | data formatting | bytes 4194304
  125.4 0.0 copy-done
  125.4 0.0 copy-start.2
  125.4 0.0 copy-start.1
  125.4 1.3 %copy.13 = bf16[1024,1024]{1,0:T(8,128)(2,1)} copy(bf16[1024,1024]{1,0:T(8,128)(2,1)S(1)} %copy-done) | data formatting | bytes 4194304
  126.8 0.0 copy-done.2
  126.8 0.7 copy.14
  127.5 0.0 copy-done.1
  127.5 0.7 copy.15
Async XLA Ops:
  122.2 3.2 %copy-start = (bf16[1024,1024]{1,0:T(8,128)(2,1)S(1)}, bf16[1024,1024]{1,0:T(8,128)(2,1)}, u32[]{:S(2)}) copy-start(bf16[1024,1024]{1,0:T(8,128)(2,1)} %get-tuple-element.9) | copy-start | bytes 6291460
  125.4 1.3 %copy-start.2 = (f32[4,64,256]{2,1,0:T(8,128)S(1)}, f32[4,64,256]{2,1,0:T(8,128)}, u32[]{:S(2)}) copy-start(f32[4,64,256]{2,1,0:T(8,128)} %get-tuple-element.10) | copy-start | bytes 786436
  125.4 2.0 %copy-start.1 = (f32[4,64,256]{2,1,0:T(8,128)S(1)}, f32[4,64,256]{2,1,0:T(8,128)}, u32[]{:S(2)}) copy-start(f32[4,64,256]{2,1,0:T(8,128)} %get-tuple-element.11) | copy-start | bytes 786436
